TPU v7x, 32 devices: a whole 2x2x4 slice. The times are simulated.
32 devices in a mesh: slab: 4 (over y, core), inner: 8 (over z, x).
Axes of the slice: x: 2, y: 2, z: 4, core: 2. Of those that a mesh axis runs over, the one named last changes fastest.
Arguments:
- x_in: bfloat16 [8192, 16384], P(('slab', 'inner')), may hold values from -6 to 6
- bc_in: bfloat16 [8192, 4096], P(('slab', 'inner')), may hold values from -6 to 6
- dt_raw: bfloat16 [8192, 256], P(('slab', 'inner')), may hold values from -6.7 to -4.3
- dt_bias: float32 [256], replicated, may hold values from -0.5 to 0.5
- a_log: float32 [256], replicated, may hold values from -8 to 0, as said below
- d_skip: float32 [256], replicated, may hold values from 0.5 to 1.5
- conv_x_weight: float32 [4, 16384], replicated, may hold values from -3 to 3
- conv_x_bias: float32 [16384], replicated, may hold values from -3 to 3
- conv_bc_weight: float32 [4, 4096], replicated, may hold values from -3 to 3
- conv_bc_bias: float32 [4096], replicated, may hold values from -3 to 3
Outputs:
- y_out: bfloat16 [8192, 16384], P('slab', 'inner')
Inputs may be any that keep to these rules, and one draw needn't show every extreme that they name: `a_log`: per-head logarithm of the decay rate.
All inputs are finite; a program needn't handle non-finite values.
Results may differ from a plain program's by a relative error of at most 0.0034.
Values may be sent and summed in bfloat16 or wider, within the bound.
No kernel may reach another device: no remote copies, remote signals or barrier semaphores. Data moves between devices by JAX's collectives and lax.ppermute only.
A program may use at most 256 MiB of HBM per device.

v0:
```python
import jax
import jax.numpy as jnp
import numpy as np
from jax import lax
from jax.sharding import PartitionSpec as P

HEADS = 256
HEADDIM = 64
STATE = 256
GROUPS = 8
CONV = 4
SPAN = 256


def from_behind(x, axis, by):
    size = lax.axis_size(axis)
    pairs = [(i, i + by) for i in range(size) if 0 <= i + by < size]
    return lax.ppermute(x, axis, pairs)


def causal_conv(row_block, before, weight, conv_bias):
    kernel_len = weight.shape[0]
    length = row_block.shape[0]
    padded = jnp.concatenate([before, row_block], axis=0).astype(jnp.float32)
    summed = conv_bias[None, :] + weight[0][None, :] * padded[0:length]
    for offset in range(1, kernel_len):
        summed = summed + weight[offset][None, :] * padded[offset : offset + length]
    return jax.nn.silu(summed).astype(jnp.bfloat16)


def head_columns(per_head, head_count):
    rows = per_head.shape[0]
    return jnp.broadcast_to(per_head[:, :, None], (rows, head_count, HEADDIM)).reshape(
        rows, head_count * HEADDIM
    )


def span_step(state, pieces):
    x_span, b_span, c_span, dt_span, da_span = pieces
    size_q = x_span.shape[0]
    head_count = dt_span.shape[1]
    cumul = jnp.cumsum(da_span, axis=0).T
    row_ids = lax.broadcasted_iota(jnp.int32, (size_q, size_q), 0)
    col_ids = lax.broadcasted_iota(jnp.int32, (size_q, size_q), 1)
    gaps = cumul[:, :, None] - cumul[:, None, :]
    decays = jnp.where((row_ids >= col_ids)[None], jnp.exp(jnp.minimum(gaps, 0.0)), 0.0)
    scores = jnp.dot(c_span, b_span.T, preferred_element_type=jnp.float32)
    mixing = (decays * scores[None] * dt_span.T[:, None, :]).astype(jnp.bfloat16)
    x_heads = x_span.reshape(size_q, head_count, HEADDIM)
    y_intra = jnp.einsum(
        "hts,shp->thp", mixing, x_heads, preferred_element_type=jnp.float32
    ).reshape(size_q, head_count * HEADDIM)
    y_inter = jnp.dot(c_span, state.astype(jnp.bfloat16), preferred_element_type=jnp.float32)
    y_inter = y_inter * head_columns(jnp.exp(cumul.T), head_count)
    weights_end = (jnp.exp(cumul[:, -1:] - cumul) * dt_span.T).T
    scaled = (x_span.astype(jnp.float32) * head_columns(weights_end, head_count)).astype(
        jnp.bfloat16
    )
    contrib = jnp.dot(b_span.T, scaled, preferred_element_type=jnp.float32)
    end_decay = head_columns(jnp.exp(cumul[:, -1])[None, :], head_count)
    new_state = end_decay * state + contrib
    return (new_state, y_intra + y_inter)


def slab_core(x_rows, b_rows, c_rows, dt_rows, da_rows):
    length = x_rows.shape[0]
    width = x_rows.shape[1]
    head_count = dt_rows.shape[1]
    span_count = length // SPAN
    inputs = (
        x_rows.reshape(span_count, SPAN, width),
        b_rows.reshape(span_count, SPAN, STATE),
        c_rows.reshape(span_count, SPAN, STATE),
        dt_rows.reshape(span_count, SPAN, head_count),
        da_rows.reshape(span_count, SPAN, head_count),
    )
    zero_state = jnp.zeros((STATE, width), jnp.float32)
    end_state, outputs = lax.scan(span_step, zero_state, inputs)
    return (outputs.reshape(length, width), end_state)


def group_copies(bc_rows, dest_group, n_inner):
    tok_rows = bc_rows.shape[0]
    split = bc_rows.reshape(tok_rows, 2, GROUPS, STATE)
    picked = jnp.take(split, dest_group, axis=2)
    return jnp.transpose(picked, (0, 2, 1, 3)).reshape(tok_rows, n_inner, 2 * STATE)


def shards(
    x_in,
    bc_in,
    dt_raw,
    dt_bias,
    a_log,
    d_skip,
    conv_x_weight,
    conv_x_bias,
    conv_bc_weight,
    conv_bc_bias,
):
    n_inner = lax.axis_size("inner")
    n_slab = lax.axis_size("slab")
    tok_dev = x_in.shape[0]
    heads_dev = HEADS // n_inner
    ch_dev = heads_dev * HEADDIM
    per_group = HEADS // GROUPS
    inner_idx = lax.axis_index("inner")
    dest_group = np.arange(n_inner) * heads_dev // per_group
    edge = CONV - 1
    dt_send = dt_raw.reshape(tok_dev, n_inner, heads_dev)
    x_prev, bc_prev = from_behind(
        (x_in[tok_dev - edge :], bc_in[tok_dev - edge :]), ("slab", "inner"), 1
    )
    x_ready = causal_conv(x_in, x_prev, conv_x_weight, conv_x_bias)
    bc_ready = causal_conv(bc_in, bc_prev, conv_bc_weight, conv_bc_bias)
    bc_send = group_copies(bc_ready, dest_group, n_inner)
    x_recv, bc_recv, dt_recv = (
        lax.all_to_all(
            x_ready.reshape(tok_dev, n_inner, ch_dev),
            "inner",
            split_axis=1,
            concat_axis=0,
            tiled=True,
        ),
        lax.all_to_all(bc_send, "inner", split_axis=1, concat_axis=0, tiled=True),
        lax.all_to_all(dt_send, "inner", split_axis=1, concat_axis=0, tiled=True),
    )
    x_slab = x_recv.reshape(-1, ch_dev)
    bc_slab = bc_recv.reshape(-1, 2 * STATE)
    bias_heads = lax.dynamic_slice_in_dim(dt_bias, inner_idx * heads_dev, heads_dev, 0)
    rate_heads = -jnp.exp(lax.dynamic_slice_in_dim(a_log, inner_idx * heads_dev, heads_dev, 0))
    skip_heads = lax.dynamic_slice_in_dim(d_skip, inner_idx * heads_dev, heads_dev, 0)
    dt_heads = jax.nn.softplus(
        dt_recv.reshape(-1, heads_dev).astype(jnp.float32) + bias_heads[None, :]
    )
    da_heads = dt_heads * rate_heads[None, :]
    c_slab = bc_slab[:, STATE:]
    y_local, end_state = slab_core(x_slab, bc_slab[:, :STATE], c_slab, dt_heads, da_heads)
    cum_slab = jnp.cumsum(da_heads, axis=0)
    slab_decay = head_columns(jnp.exp(cum_slab[-1:]), heads_dev)[0]
    incoming = jnp.zeros_like(end_state)
    outgoing = end_state
    for hop_number in range(n_slab - 1):
        incoming = from_behind(outgoing, "slab", 1)
        outgoing = slab_decay[None, :] * incoming + end_state
    carried = jnp.dot(c_slab, incoming.astype(jnp.bfloat16), preferred_element_type=jnp.float32)
    carried = carried * head_columns(jnp.exp(cum_slab), heads_dev)
    skip_cols = jnp.repeat(skip_heads, HEADDIM)
    y_slab = y_local + carried + skip_cols[None, :] * x_slab.astype(jnp.float32)
    return y_slab.astype(jnp.bfloat16)


def solution(mesh):
    placed = (
        P(("slab", "inner"), None),
        P(("slab", "inner"), None),
        P(("slab", "inner"), None),
        P(),
        P(),
        P(),
        P(),
        P(),
        P(),
        P(),
    )
    return jax.shard_map(
        shards, mesh=mesh, in_specs=placed, out_specs=P("slab", "inner"), check_vma=False
    )
```

profile of v0, /device:TPU:0, one launch (start us, length us, event | category | flops | bytes accessed | tf_op | source)
XLA Modules:
  0.0 606.8 jit_solution(15291614099124217635)
XLA Ops:
  1.7 7.3 %all-to-all-start = ((bf16[256,8,32]{0,2,1:T(8,128)(2,1)}), bf16[256,8,32]{0,2,1:T(8,128)(2,1)S(1)}, u32[]{:S(2)}, u32[]{:S(2)}) async-start(bf16[256,8,32]{0,2,1:T(8,128)(2,1)} %bitcast), calls=%async_computation | async-start | bytes 262144 | tf_op jit(solution)/shard_map/all_to_all | solution.py:126
  9.8 4.5 collective-permute-start
  29.7 7.0 %multiply_convert_fusion.4 = bf16[256,4096]{0,1:T(8,128)(2,1)S(1)} fusion(f32[259,4096]{0,1:T(8,128)S(1)} %maximum_convert_fusion.1, f32[4096]{0:T(1024)S(1)} %bitcast.210, f32[4096]{0:T(1024)S(1)} %bitcast.211, f32[4096]{0:T(1024)S(1)} %bitcast.209, f32[4096]{0:T(1024)S(1)} %bitcast.208, f32[4096]{0:T(1024)S(1)} %copy-done.6), kind=kLoop, calls=%fused_computation.66 | loop fusion | flops 13631488 | bytes 18956288 | tf_op jit(solution)/shard_map/convert_element_type | solution.py:28
  47.0 11.8 %maximum_convert_fusion = f32[259,16384]{1,0:T(8,128)} fusion(bf16[256,16384]{1,0:T(8,128)(2,1)} %param.13, bf16[3,16384]{1,0:T(4,128)(2,1)} %collective-permute-done.1), kind=kLoop, calls=%fused_computation.56 | loop fusion | flops 16973824 | bytes 25460736 | tf_op jit(solution)/shard_map/convert_element_type | solution.py:24
  58.8 4.0 all-to-all-start.1
  62.8 27.1 %multiply_convert_fusion.3 = bf16[256,16384]{1,0:T(8,128)(2,1)} fusion(f32[259,16384]{1,0:T(8,128)} %maximum_convert_fusion, f32[16384]{0:T(1024)S(1)} %bitcast.204, f32[16384]{0:T(1024)S(1)} %bitcast.205, f32[16384]{0:T(1024)S(1)} %bitcast.203, f32[16384]{0:T(1024)S(1)} %bitcast.202, f32[16384]{0:T(1024)S(1)} %copy-done.5), kind=kLoop, calls=%fused_computation.55 | loop fusion | flops 54525952 | bytes 75825152 | tf_op jit(solution)/shard_map/convert_element_type | solution.py:28
  89.9 11.9 %copy.96 = bf16[256,16384]{0,1:T(8,128)(2,1)} copy(bf16[256,16384]{1,0:T(8,128)(2,1)} %multiply_convert_fusion.3) | data formatting | bytes 16777216 | tf_op jit(solution)/shard_map/convert_element_type | solution.py:28
  101.9 10.6 %all-to-all-done.1 = bf16[256,8,512]{0,2,1:T(8,128)(2,1)S(1)} async-done(((bf16[256,8,512]{0,2,1:T(8,128)(2,1)}), bf16[256,8,512]{0,2,1:T(8,128)(2,1)S(1)}, u32[]{:S(2)}, u32[]{:S(2)}) %all-to-all-start.1) | async-done | bytes 2097184 | tf_op jit(solution)/shard_map/all_to_all | solution.py:125
  113.7 5.1 all-to-all-start.2
  127.1 175.1 %all-to-all-done.2 = bf16[256,8,2048]{0,2,1:T(8,128)(2,1)} async-done(((bf16[256,8,2048]{0,2,1:T(8,128)(2,1)}), bf16[256,8,2048]{0,2,1:T(8,128)(2,1)}, u32[]{:S(2)}, u32[]{:S(2)}) %all-to-all-start.2) | async-done | bytes 8388640 | tf_op jit(solution)/shard_map/all_to_all | solution.py:118
  302.1 194.8 %while.13 = (s32[]{:T(128)}, f32[256,2048]{1,0:T(8,128)S(1)}, f32[8,256,2048]{2,1,0:T(8,128)}, f32[8,256,32]{1,2,0:T(8,128)}, bf16[8,256,256]{2,1,0:T(8,128)(2,1...) while((s32[]{:T(128)}, f32[256,2048]{1,0:T(8,128)S(1)}, ...), condition=%wide.region_3.4_spmd.clone, body=%wide.region_0.3_spmd.clone.sunk | while | flops 857301120 | bytes 33167368 | solution.py:78
  307.3 4.2 fusion.72
  318.8 4.1 fusion.73
  331.7 4.2 fusion.72
  356.0 4.2 fusion.72
  367.5 4.0 fusion.73
  380.4 4.2 fusion.72
  391.9 4.1 fusion.73
  404.7 4.2 fusion.72
  416.2 4.1 fusion.73
  429.1 4.2 fusion.72
  440.6 4.0 fusion.73
  453.4 4.2 fusion.72
  465.0 4.0 fusion.73
  477.8 4.2 fusion.72
  499.9 9.1 %reduce-window.16 = f32[32,16,128]{2,1,0:T(8,128)S(1)} reduce-window(f32[32,16,128]{2,1,0:T(8,128)S(1)} %bitcast.199, f32[]{:T(128)} %constant.44.clone.1), window={size=1x1x128 pad=0_0x0_0x127_0}, to_apply=%region_4.5 | reduce-window | flops 8323072 | bytes 524292 | tf_op jit(solution)/shard_map/reduce-window.2
  513.4 14.0 %collective-permute-start.3 = (f32[256,2048]{1,0:T(8,128)}, f32[256,2048]{1,0:T(8,128)}, u32[]{:S(2)}, u32[]{:S(2)}) collective-permute-start(f32[256,2048]{1,0:T(8,128)} %multiply_add_fusion.1), channel_id=1, source_target_pairs={{0,8},{8,16},{16,24},{1,9},{9,17},{17,25},{2,10},{10,18},{18,26},{... | collective-permute-start | bytes 6291464 | tf_op jit(solution)/shard_map/ppermute | solution.py:18
  527.7 7.8 %broadcast_in_dim.88 = f32[2048,32,64]{0,2,1:T(8,128)} broadcast(f32[2048,32]{0,1:T(8,128)S(1)} %fusion.47), dimensions={0,1} | broadcast | bytes 17039360 | tf_op jit(solution)/shard_map/broadcast_in_dim | solution.py:33
  535.6 17.6 %copy.100 = f32[2048,2048]{1,0:T(8,128)} copy(f32[2048,2048]{0,1:T(8,128)} %bitcast.189) | data formatting | bytes 33554432 | tf_op jit(solution)/shard_map/reshape | solution.py:33
  559.3 10.6 %bitcast_convert_fusion = f32[8,256,1,2048]{1,3,0,2:T(8,128)} fusion(bf16[256,8,2048]{0,2,1:T(8,128)(2,1)} %all-to-all-done.2), kind=kLoop, calls=%fused_computation.57 | loop fusion | flops 4194304 | bytes 25165824 | tf_op jit(solution)/shard_map/convert_element_type | solution.py:149
  569.9 16.6 %copy.101 = f32[8,256,1,2048]{3,1,0,2:T(8,128)} copy(f32[8,256,1,2048]{1,3,0,2:T(8,128)} %bitcast_convert_fusion) | data formatting | bytes 33554432 | tf_op jit(solution)/shard_map/convert_element_type | solution.py:149
  586.5 20.3 %fusion.31 = bf16[2048,2048]{1,0:T(8,128)(2,1)} fusion(f32[8,256,1,2048]{3,1,0,2:T(8,128)} %copy.101, f32[8,256,2048]{2,1,0:T(8,128)} %get-tuple-element.48, f32[2048,2048]{1,0:T(8,128)} %copy.100, f32[2048]{0:T(1024)S(1)} %mul.208, bf16[256,2048]{1,0:T(8,128)(2,1)S(1)} %collective-permute-done.4, bf16[2048,512]{1,0:T(8,128)(2,1)S(1)} %bitcast.193), kind=kOutput, calls=%fused_computation.53 | convolution fusion | flops 2168455168 | bytes 60825600 | tf_op jit(solution)/shard_map/dot_general | solution.py:146
  (225 shorter events, 187.8 us)
Async XLA Ops:
  1.7 57.1 %all-to-all-start = ((bf16[256,8,32]{0,2,1:T(8,128)(2,1)}), bf16[256,8,32]{0,2,1:T(8,128)(2,1)S(1)}, u32[]{:S(2)}, u32[]{:S(2)}) async-start(bf16[256,8,32]{0,2,1:T(8,128)(2,1)} %bitcast), calls=%async_computation | async-start | bytes 262144 | tf_op jit(solution)/shard_map/all_to_all | solution.py:126
  9.8 17.2 %collective-permute-start = (bf16[3,4096]{1,0:T(4,128)(2,1)S(1)}, bf16[3,4096]{1,0:T(4,128)(2,1)}, u32[]{:S(2)}, u32[]{:S(2)}) collective-permute-start(bf16[3,4096]{1,0:T(4,128)(2,1)S(1)} %slice.80), channel_id=1, source_target_pairs={{0,1},{1,2},{2,3},{3,4},{4,5},{5,6},{6,7},{7,8},{8,9},{9,10},{10,1... | collective-permute-start | bytes 73736 | tf_op jit(solution)/shard_map/ppermute | solution.py:18
  16.0 31.0 %collective-permute-start.1 = (bf16[3,16384]{1,0:T(4,128)(2,1)}, bf16[3,16384]{1,0:T(4,128)(2,1)}, u32[]{:S(2)}, u32[]{:S(2)}) collective-permute-start(bf16[3,16384]{1,0:T(4,128)(2,1)} %slice.90), channel_id=1, source_target_pairs={{0,1},{1,2},{2,3},{3,4},{4,5},{5,6},{6,7},{7,8},{8,9},{9,10},{10,1... | collective-permute-start | bytes 294920 | tf_op jit(solution)/shard_map/ppermute | solution.py:18
  28.3 1.4 copy-start.2
  28.3 1.4 copy-start.3
  28.3 1.4 copy-start.4
  28.3 1.4 copy-start.6
  36.7 4.8 copy-start.7
  58.8 4.0 copy-start.5
  58.8 53.6 %all-to-all-start.1 = ((bf16[256,8,512]{0,2,1:T(8,128)(2,1)}), bf16[256,8,512]{0,2,1:T(8,128)(2,1)S(1)}, u32[]{:S(2)}, u32[]{:S(2)}) async-start(bf16[256,8,512]{0,2,1:T(8,128)(2,1)} %bitcast.195), calls=%async_computation.1 | async-start | bytes 4194304 | tf_op jit(solution)/shard_map/all_to_all | solution.py:125
  112.4 1.3 copy-start.1
  112.4 6.5 %copy-start.8 = (f32[256]{0:T(256)S(1)}, f32[256]{0:T(256)}, u32[]{:S(2)}) copy-start(f32[256]{0:T(256)} %param.16) | copy-start | bytes 3076
  112.4 6.6 %copy-start.9 = (f32[256]{0:T(256)S(1)}, f32[256]{0:T(256)}, u32[]{:S(2)}) copy-start(f32[256]{0:T(256)} %param.17) | copy-start | bytes 3076
  113.7 188.4 %all-to-all-start.2 = ((bf16[256,8,2048]{0,2,1:T(8,128)(2,1)}), bf16[256,8,2048]{0,2,1:T(8,128)(2,1)}, u32[]{:S(2)}, u32[]{:S(2)}) async-start(bf16[256,8,2048]{0,2,1:T(8,128)(2,1)} %bitcast.191), calls=%async_computation.2 | async-start | bytes 16777216 | tf_op jit(solution)/shard_map/all_to_all | solution.py:118
  496.9 13.2 %collective-permute-start.2 = (f32[256,2048]{1,0:T(8,128)S(1)}, f32[256,2048]{1,0:T(8,128)}, u32[]{:S(2)}, u32[]{:S(2)}) collective-permute-start(f32[256,2048]{1,0:T(8,128)S(1)} %get-tuple-element.49), channel_id=1, source_target_pairs={{0,8},{8,16},{16,24},{1,9},{9,17},{17,25},{2,10},{10,18},{18,26},{... | collective-permute-start | bytes 6291464 | tf_op jit(solution)/shard_map/ppermute | solution.py:18
  509.0 18.4 %copy-start.10 = (f32[256]{0:T(256)S(1)}, f32[256]{0:T(256)}, u32[]{:S(2)}) copy-start(f32[256]{0:T(256)} %param.18) | copy-start | bytes 3076
  513.4 39.8 %collective-permute-start.3 = (f32[256,2048]{1,0:T(8,128)}, f32[256,2048]{1,0:T(8,128)}, u32[]{:S(2)}, u32[]{:S(2)}) collective-permute-start(f32[256,2048]{1,0:T(8,128)} %multiply_add_fusion.1), channel_id=1, source_target_pairs={{0,8},{8,16},{16,24},{1,9},{9,17},{17,25},{2,10},{10,18},{18,26},{... | collective-permute-start | bytes 6291464 | tf_op jit(solution)/shard_map/ppermute | solution.py:18
  556.1 30.4 %collective-permute-start.4 = (bf16[256,2048]{1,0:T(8,128)(2,1)}, bf16[256,2048]{1,0:T(8,128)(2,1)S(1)}, u32[]{:S(2)}, u32[]{:S(2)}) collective-permute-start(bf16[256,2048]{1,0:T(8,128)(2,1)} %multiply_add_fusion), channel_id=1, source_target_pairs={{0,8},{8,16},{16,24},{1,9},{9,17},{17,25},{2,10},{10,18},{18,26},{... | collective-permute-start | bytes 3145736 | tf_op jit(solution)/shard_map/ppermute | solution.py:18
  569.9 16.6 %copy-start = (bf16[8,256,1,512]{3,1,0,2:T(8,128)(2,1)S(1)}, bf16[8,256,1,512]{3,1,0,2:T(8,128)(2,1)}, u32[]{:S(2)}) copy-start(bf16[8,256,1,512]{3,1,0,2:T(8,128)(2,1)} %copy.95) | copy-start | bytes 6291460
where the time goes:
time: 611 us; the launch traced here: 607 us
  waiting for transfers between devices  186 us (30%)
  local copies, waits for them, and re-layouts  163 us (27%)
  matrix products  113 us (18%)
  other arithmetic  99.8 us (16%)
  starting transfers between devices  44.3 us (7%)
    all_to_all x1, waiting for transfers between devices, shards(): lax.all_to_all(x_ready.reshape(tok_dev, n_inner, ch_dev), 'inner', split_...  175 us
    reshape x9, local copies, waits for them, and re-layouts, head_columns(): jnp.broadcast_to(per_head[:, :, None], (rows, head_count, HEADDIM))  40.8 us
    convert_element_type x2, other arithmetic, causal_conv(): return jax.nn.silu(summed).astype(jnp.bfloat16)  34.1 us
    dot_general x8, matrix products, span_step(): jnp.einsum('hts,shp->thp', mixing, x_heads, preferred_element_type=jnp.fl...  33.6 us
    dot_general x8, matrix products, span_step(): jnp.dot(c_span, state.astype(jnp.bfloat16), preferred_element_type=jnp.fl...  32.4 us
    ppermute x5, starting transfers between devices, from_behind(): return lax.ppermute(x, axis, pairs)  27.8 us
    reshape x8, local copies, waits for them, and re-layouts, span_step(): y_intra = jnp.einsum('hts,shp->thp', mixing, x_heads, preferred_element_t...  23.5 us
    broadcast_in_dim x27, local copies, waits for them, and re-layouts, head_columns(): jnp.broadcast_to(per_head[:, :, None], (rows, head_count, HEADDIM))  21 us
  transfers between devices with their start and end apart: 8, of which 2 were waited for; matrix products, arithmetic and copies ran while one was open for 25% of the time, Pallas kernels for 0%

commit v1 on v0

--- a/solution.py
+++ b/solution.py
@@ -115,12 +115,18 @@
     bc_ready = causal_conv(bc_in, bc_prev, conv_bc_weight, conv_bc_bias)
     bc_send = group_copies(bc_ready, dest_group, n_inner)
     x_recv, bc_recv, dt_recv = (
-        lax.all_to_all(
-            x_ready.reshape(tok_dev, n_inner, ch_dev),
-            "inner",
-            split_axis=1,
-            concat_axis=0,
-            tiled=True,
+        jnp.concatenate(
+            lax.all_to_all(
+                jnp.stack(
+                    jnp.split(
+                        x_ready.reshape(tok_dev, n_inner, ch_dev), lax.axis_size("inner"), axis=1
+                    )
+                ),
+                "inner",
+                0,
+                0,
+            ),
+            axis=0,
         ),
         lax.all_to_all(bc_send, "inner", split_axis=1, concat_axis=0, tiled=True),
         lax.all_to_all(dt_send, "inner", split_axis=1, concat_axis=0, tiled=True),

time: 611 us -> 656 us (1.074)
  waiting for transfers between devices: 186 us -> 213 us
  starting transfers between devices: 44.3 us -> 63.4 us
  other arithmetic: 99.8 us -> 86.2 us
  local copies, waits for them, and re-layouts: 163 us -> 174 us
    all_to_all x1, waiting for transfers between devices: 10.6 us -> 34.9 us  [shards(): lax.all_to_all(bc_send, 'inner', split_axis=1, concat_axis=0, tiled=True)]
    ppermute x5, starting transfers between devices: 27.8 us -> 50.1 us  [from_behind(): return lax.ppermute(x, axis, pairs)]
    unnamed x27 -> x36, local copies, waits for them, and re-layouts: 6.42 us -> 19.4 us
    convert_element_type x1 -> x0, other arithmetic: 10.6 us -> none  [shards(): y_slab = y_local + carried + skip_cols[None, :] * x_slab.astype(jnp.float32)]
  transfers between devices with their start and end apart: 8 -> 8, of which waited for: 2 -> 3; matrix products, arithmetic and copies ran while one was open for 25% -> 23% of each run, Pallas kernels for 0% -> 0%
where the time goes in v1:
time: 656 us; the launch traced here: 651 us
  waiting for transfers between devices  213 us (32%)
  local copies, waits for them, and re-layouts  174 us (27%)
  matrix products  114 us (17%)
  other arithmetic  86.2 us (13%)
  starting transfers between devices  63.4 us (10%)
    all_to_all x1, waiting for transfers between devices, shards(): lax.all_to_all(jnp.stack(jnp.split(x_ready.reshape(tok_dev, n_inner, ch_d...  175 us
    ppermute x5, starting transfers between devices, from_behind(): return lax.ppermute(x, axis, pairs)  50.1 us
    reshape x9, local copies, waits for them, and re-layouts, head_columns(): jnp.broadcast_to(per_head[:, :, None], (rows, head_count, HEADDIM))  40.8 us
    all_to_all x1, waiting for transfers between devices, shards(): lax.all_to_all(bc_send, 'inner', split_axis=1, concat_axis=0, tiled=True)  34.9 us
    convert_element_type x2, other arithmetic, causal_conv(): return jax.nn.silu(summed).astype(jnp.bfloat16)  34.1 us
    dot_general x8, matrix products, span_step(): jnp.einsum('hts,shp->thp', mixing, x_heads, preferred_element_type=jnp.fl...  33.6 us
    dot_general x8, matrix products, span_step(): jnp.dot(c_span, state.astype(jnp.bfloat16), preferred_element_type=jnp.fl...  32.4 us
    reshape x8, local copies, waits for them, and re-layouts, span_step(): y_intra = jnp.einsum('hts,shp->thp', mixing, x_heads, preferred_element_t...  23.5 us
  transfers between devices with their start and end apart: 8, of which 3 were waited for; matrix products, arithmetic and copies ran while one was open for 23% of the time, Pallas kernels for 0%

profile of v1, /device:TPU:0, one launch (start us, length us, event | category | flops | bytes accessed | tf_op | source)
XLA Modules:
  0.0 650.8 jit_solution(14489552291728759186)
XLA Ops:
  1.7 5.5 collective-permute-start.1
  8.8 4.2 all-to-all-start
  13.9 4.5 collective-permute-start
  28.9 7.0 %multiply_convert_fusion.4 = bf16[256,4096]{0,1:T(8,128)(2,1)S(1)} fusion(f32[259,4096]{0,1:T(8,128)S(1)} %maximum_convert_fusion.1, f32[4096]{0:T(1024)S(1)} %bitcast.244, f32[4096]{0:T(1024)S(1)} %bitcast.245, f32[4096]{0:T(1024)S(1)} %bitcast.243, f32[4096]{0:T(1024)S(1)} %bitcast.242, f32[4096]{0:T(1024)S(1)} %copy-done.7), kind=kLoop, calls=%fused_computation.65 | loop fusion | flops 13631488 | bytes 18956288 | tf_op jit(solution)/shard_map/convert_element_type | solution.py:28
  46.2 11.8 %maximum_convert_fusion = f32[259,16384]{1,0:T(8,128)} fusion(bf16[256,16384]{1,0:T(8,128)(2,1)} %param.13, bf16[3,16384]{1,0:T(4,128)(2,1)} %collective-permute-done.1), kind=kLoop, calls=%fused_computation.56 | loop fusion | flops 16973824 | bytes 25460736 | tf_op jit(solution)/shard_map/convert_element_type | solution.py:24
  58.0 27.1 %multiply_convert_fusion.3 = bf16[256,16384]{1,0:T(8,128)(2,1)} fusion(f32[259,16384]{1,0:T(8,128)} %maximum_convert_fusion, f32[16384]{0:T(1024)S(1)} %bitcast.238, f32[16384]{0:T(1024)S(1)} %bitcast.239, f32[16384]{0:T(1024)S(1)} %bitcast.237, f32[16384]{0:T(1024)S(1)} %bitcast.236, f32[16384]{0:T(1024)S(1)} %copy-done.6), kind=kLoop, calls=%fused_computation.55 | loop fusion | flops 54525952 | bytes 75825152 | tf_op jit(solution)/shard_map/convert_element_type | solution.py:28
  85.1 12.0 %copy.117 = bf16[256,16384]{0,1:T(8,128)(2,1)} copy(bf16[256,16384]{1,0:T(8,128)(2,1)} %multiply_convert_fusion.3) | data formatting | bytes 16777216 | tf_op jit(solution)/shard_map/convert_element_type | solution.py:28
  115.1 34.9 %all-to-all-done.1 = bf16[256,8,512]{0,2,1:T(8,128)(2,1)S(1)} async-done(((bf16[256,8,512]{0,2,1:T(8,128)(2,1)}), bf16[256,8,512]{0,2,1:T(8,128)(2,1)S(1)}, u32[]{:S(2)}, u32[]{:S(2)}) %all-to-all-start.1) | async-done | bytes 2097184 | tf_op jit(solution)/shard_map/all_to_all | solution.py:131
  151.3 5.1 all-to-all-start.2
  164.6 174.5 %all-to-all-done.2 = bf16[8,256,1,2048]{1,3,2,0:T(8,128)(2,1)} async-done(((bf16[8,256,1,2048]{1,3,2,0:T(8,128)(2,1)}), bf16[8,256,1,2048]{1,3,2,0:T(8,128)(2,1)}, u32[]{:S(2)}, u32[]{:S(2)}) %all-to-all-start.2) | async-done | bytes 8388640 | tf_op jit(solution)/shard_map/all_to_all | solution.py:119
  339.2 194.7 %while.13 = (s32[]{:T(128)}, f32[256,2048]{1,0:T(8,128)S(1)}, f32[8,256,2048]{2,1,0:T(8,128)}, f32[8,256,32]{1,2,0:T(8,128)}, bf16[8,256,256]{2,1,0:T(8,128)(2,1...) while((s32[]{:T(128)}, f32[256,2048]{1,0:T(8,128)S(1)}, ...), condition=%wide.region_3.4_spmd.clone, body=%wide.region_0.3_spmd.clone.sunk | while | flops 857301120 | bytes 33167368 | solution.py:78
  344.4 4.2 fusion.80
  355.9 4.1 fusion.81
  368.7 4.2 fusion.80
  393.0 4.2 fusion.80
  404.5 4.0 fusion.81
  417.4 4.2 fusion.80
  428.9 4.1 fusion.81
  441.7 4.2 fusion.80
  453.2 4.1 fusion.81
  466.1 4.2 fusion.80
  477.6 4.0 fusion.81
  490.4 4.2 fusion.80
  501.9 4.0 fusion.81
  514.8 4.2 fusion.80
  536.8 9.1 %reduce-window.16 = f32[32,16,128]{2,1,0:T(8,128)S(1)} reduce-window(f32[32,16,128]{2,1,0:T(8,128)S(1)} %bitcast.233, f32[]{:T(128)} %constant.44.clone.1), window={size=1x1x128 pad=0_0x0_0x127_0}, to_apply=%region_4.5 | reduce-window | flops 8323072 | bytes 524292 | tf_op jit(solution)/shard_map/reduce-window.2
  549.0 12.8 %collective-permute-start.3 = (f32[256,2048]{1,0:T(8,128)S(1)}, f32[256,2048]{1,0:T(8,128)S(1)}, u32[]{:S(2)}, u32[]{:S(2)}) collective-permute-start(f32[256,2048]{1,0:T(8,128)S(1)} %multiply_add_fusion.1), channel_id=1, source_target_pairs={{0,8},{8,16},{16,24},{1,9},{9,17},{17,25},{2,10},{10,18},{18,26},{... | collective-permute-start | bytes 6291464 | tf_op jit(solution)/shard_map/ppermute | solution.py:18
  566.8 24.7 %collective-permute-start.4 = (bf16[256,2048]{1,0:T(8,128)(2,1)}, bf16[256,2048]{1,0:T(8,128)(2,1)}, u32[]{:S(2)}, u32[]{:S(2)}) collective-permute-start(bf16[256,2048]{1,0:T(8,128)(2,1)} %multiply_add_fusion), channel_id=1, source_target_pairs={{0,8},{8,16},{16,24},{1,9},{9,17},{17,25},{2,10},{10,18},{18,26},{... | collective-permute-start | bytes 3145736 | tf_op jit(solution)/shard_map/ppermute | solution.py:18
  591.7 7.9 %broadcast_in_dim.88 = f32[2048,32,64]{0,2,1:T(8,128)} broadcast(f32[2048,32]{0,1:T(8,128)S(1)} %fusion.55), dimensions={0,1} | broadcast | bytes 17039360 | tf_op jit(solution)/shard_map/broadcast_in_dim | solution.py:33
  599.6 17.7 %copy.121 = f32[2048,2048]{1,0:T(8,128)} copy(f32[2048,2048]{0,1:T(8,128)} %bitcast.216) | data formatting | bytes 33554432 | tf_op jit(solution)/shard_map/reshape | solution.py:33
  617.3 12.9 %copy.122 = f32[8,256,1,2048]{3,1,0,2:T(8,128)} copy(bf16[8,256,1,2048]{1,3,2,0:T(8,128)(2,1)} %all-to-all-done.2) | data formatting | bytes 25165824 | tf_op jit(solution)/shard_map/convert_element_type | solution.py:155
  630.2 20.6 %fusion.31 = bf16[2048,2048]{1,0:T(8,128)(2,1)} fusion(f32[8,256,1,2048]{3,1,0,2:T(8,128)} %copy.122, f32[8,256,2048]{2,1,0:T(8,128)} %get-tuple-element.48, f32[2048,2048]{1,0:T(8,128)} %copy.121, f32[2048]{0:T(1024)S(1)} %mul.208, bf16[256,2048]{1,0:T(8,128)(2,1)} %collective-permute-done.4, bf16[2048,512]{1,0:T(8,128)(2,1)S(1)} %bitcast.227), kind=kOutput, calls=%fused_computation.53 | convolution fusion | flops 2168455168 | bytes 60825600 | tf_op jit(solution)/shard_map/dot_general | solution.py:152
  (234 shorter events, 199.9 us)
Async XLA Ops:
  1.7 44.5 %collective-permute-start.1 = (bf16[3,16384]{1,0:T(4,128)(2,1)}, bf16[3,16384]{1,0:T(4,128)(2,1)}, u32[]{:S(2)}, u32[]{:S(2)}) collective-permute-start(bf16[3,16384]{1,0:T(4,128)(2,1)} %slice.90), channel_id=1, source_target_pairs={{0,1},{1,2},{2,3},{3,4},{4,5},{5,6},{6,7},{7,8},{8,9},{9,10},{10,1... | collective-permute-start | bytes 294920 | tf_op jit(solution)/shard_map/ppermute | solution.py:18
  8.8 88.3 %all-to-all-start = ((bf16[256,8,32]{0,2,1:T(8,128)(2,1)}), bf16[256,8,32]{0,2,1:T(8,128)(2,1)S(1)}, u32[]{:S(2)}, u32[]{:S(2)}) async-start(bf16[256,8,32]{0,2,1:T(8,128)(2,1)} %bitcast), calls=%async_computation | async-start | bytes 262144 | tf_op jit(solution)/shard_map/all_to_all | solution.py:132
  13.9 12.3 %collective-permute-start = (bf16[3,4096]{1,0:T(4,128)(2,1)S(1)}, bf16[3,4096]{1,0:T(4,128)(2,1)}, u32[]{:S(2)}, u32[]{:S(2)}) collective-permute-start(bf16[3,4096]{1,0:T(4,128)(2,1)S(1)} %slice.80), channel_id=1, source_target_pairs={{0,1},{1,2},{2,3},{3,4},{4,5},{5,6},{6,7},{7,8},{8,9},{9,10},{10,1... | collective-permute-start | bytes 73736 | tf_op jit(solution)/shard_map/ppermute | solution.py:18
  27.5 1.4 copy-start.3
  27.5 1.4 copy-start.4
  27.5 1.4 copy-start.5
  27.5 1.4 copy-start.7
  35.9 4.8 copy-start.8
  46.2 11.8 %copy-start.6 = (f32[16384]{0:T(1024)S(1)}, f32[16384]{0:T(1024)}, u32[]{:S(2)}) copy-start(f32[16384]{0:T(1024)} %param.20) | copy-start | bytes 196612
  97.1 52.9 %all-to-all-start.1 = ((bf16[256,8,512]{0,2,1:T(8,128)(2,1)}), bf16[256,8,512]{0,2,1:T(8,128)(2,1)S(1)}, u32[]{:S(2)}, u32[]{:S(2)}) async-start(bf16[256,8,512]{0,2,1:T(8,128)(2,1)} %bitcast.229), calls=%async_computation.1 | async-start | bytes 4194304 | tf_op jit(solution)/shard_map/all_to_all | solution.py:131
  101.1 9.9 %copy-start = (bf16[256,16384]{0,1:T(8,128)(2,1)S(1)}, bf16[256,16384]{0,1:T(8,128)(2,1)}, u32[]{:S(2)}) copy-start(bf16[256,16384]{0,1:T(8,128)(2,1)} %copy.117) | copy-start | bytes 25165828
  115.1 41.4 %copy-start.9 = (f32[256]{0:T(256)S(1)}, f32[256]{0:T(256)}, u32[]{:S(2)}) copy-start(f32[256]{0:T(256)} %param.16) | copy-start | bytes 3076
  115.1 41.5 %copy-start.10 = (f32[256]{0:T(256)S(1)}, f32[256]{0:T(256)}, u32[]{:S(2)}) copy-start(f32[256]{0:T(256)} %param.17) | copy-start | bytes 3076
  150.0 1.3 copy-start.2
  151.3 187.8 %all-to-all-start.2 = ((bf16[8,256,1,2048]{1,3,2,0:T(8,128)(2,1)}), bf16[8,256,1,2048]{1,3,2,0:T(8,128)(2,1)}, u32[]{:S(2)}, u32[]{:S(2)}) async-start(bf16[8,256,1,2048]{1,3,2,0:T(8,128)(2,1)} %fusion.36), calls=%async_computation.2 | async-start | bytes 16777216 | tf_op jit(solution)/shard_map/all_to_all | solution.py:119
  533.9 57.6 %copy-start.11 = (f32[256]{0:T(256)S(1)}, f32[256]{0:T(256)}, u32[]{:S(2)}) copy-start(f32[256]{0:T(256)} %param.18) | copy-start | bytes 3076
  533.9 13.2 %collective-permute-start.2 = (f32[256,2048]{1,0:T(8,128)S(1)}, f32[256,2048]{1,0:T(8,128)}, u32[]{:S(2)}, u32[]{:S(2)}) collective-permute-start(f32[256,2048]{1,0:T(8,128)S(1)} %get-tuple-element.49), channel_id=1, source_target_pairs={{0,8},{8,16},{16,24},{1,9},{9,17},{17,25},{2,10},{10,18},{18,26},{... | collective-permute-start | bytes 6291464 | tf_op jit(solution)/shard_map/ppermute | solution.py:18
  549.0 16.4 %collective-permute-start.3 = (f32[256,2048]{1,0:T(8,128)S(1)}, f32[256,2048]{1,0:T(8,128)S(1)}, u32[]{:S(2)}, u32[]{:S(2)}) collective-permute-start(f32[256,2048]{1,0:T(8,128)S(1)} %multiply_add_fusion.1), channel_id=1, source_target_pairs={{0,8},{8,16},{16,24},{1,9},{9,17},{17,25},{2,10},{10,18},{18,26},{... | collective-permute-start | bytes 6291464 | tf_op jit(solution)/shard_map/ppermute | solution.py:18
  566.8 63.5 %collective-permute-start.4 = (bf16[256,2048]{1,0:T(8,128)(2,1)}, bf16[256,2048]{1,0:T(8,128)(2,1)}, u32[]{:S(2)}, u32[]{:S(2)}) collective-permute-start(bf16[256,2048]{1,0:T(8,128)(2,1)} %multiply_add_fusion), channel_id=1, source_target_pairs={{0,8},{8,16},{16,24},{1,9},{9,17},{17,25},{2,10},{10,18},{18,26},{... | collective-permute-start | bytes 3145736 | tf_op jit(solution)/shard_map/ppermute | solution.py:18
  617.3 13.0 %copy-start.1 = (bf16[8,256,1,512]{3,1,0,2:T(8,128)(2,1)S(1)}, bf16[8,256,1,512]{3,1,0,2:T(8,128)(2,1)}, u32[]{:S(2)}) copy-start(bf16[8,256,1,512]{3,1,0,2:T(8,128)(2,1)} %copy.116) | copy-start | bytes 6291460
